TPU v7x, 32 devices: a whole 2x2x4 slice. The times are simulated.
32 devices in a mesh: seq: 2 (over y), ctx: 4 (over z), tp: 4 (over x, core).
Axes of the slice: x: 2, y: 2, z: 4, core: 2. Of those that a mesh axis runs over, the one named last changes fastest.
Arguments:
- tokens: bfloat16 [2048, 2048], P(('seq', 'ctx')), may hold values from -6 to 6
- query_weight: bfloat16 [2048, 2048], P(('seq', 'ctx'), 'tp'), may hold values from -0.125 to 0.125
- key_weight: bfloat16 [2048, 2048], P(('seq', 'ctx'), 'tp'), may hold values from -0.125 to 0.125
- value_weight: bfloat16 [2048, 2048], P(('seq', 'ctx'), 'tp'), may hold values from -0.125 to 0.125
- output_weight: bfloat16 [2048, 2048], P('tp', ('seq', 'ctx')), may hold values from -1.5 to 1.5
- gate_weight: bfloat16 [2048, 8192], P(('seq', 'ctx'), 'tp'), may hold values from -0.125 to 0.125
- up_weight: bfloat16 [2048, 8192], P(('seq', 'ctx'), 'tp'), may hold values from -0.125 to 0.125
- down_weight: bfloat16 [8192, 2048], P('tp', ('seq', 'ctx')), may hold values from -0.0625 to 0.0625
- attention_gain: bfloat16 [2048], P(('seq', 'ctx')), may hold values from 0.25 to 1.75
- feedforward_gain: bfloat16 [2048], P(('seq', 'ctx')), may hold values from 0.25 to 1.75
- order: int32 [8], replicated, may hold values from 0 to 7, each once
- cotangent: bfloat16 [2048, 2048], P(('seq', 'ctx')), may hold values from -6 to 6
Outputs:
- block_output: bfloat16 [2048, 2048], P(('seq', 'ctx'))
- input_grad: float32 [2048, 2048], P(('seq', 'ctx'))
- query_weight_grad: float32 [2048, 2048], P(('seq', 'ctx'), 'tp')
- key_weight_grad: float32 [2048, 2048], P(('seq', 'ctx'), 'tp')
- value_weight_grad: float32 [2048, 2048], P(('seq', 'ctx'), 'tp')
- output_weight_grad: float32 [2048, 2048], P('tp', ('seq', 'ctx'))
- gate_weight_grad: float32 [2048, 8192], P(('seq', 'ctx'), 'tp')
- up_weight_grad: float32 [2048, 8192], P(('seq', 'ctx'), 'tp')
- down_weight_grad: float32 [8192, 2048], P('tp', ('seq', 'ctx'))
- attention_gain_grad: float32 [2048], P(('seq', 'ctx'))
- feedforward_gain_grad: float32 [2048], P(('seq', 'ctx'))
Inputs may be any that keep to these rules, and one draw needn't show every extreme that they name: order holds every block position of a sequence once; the device of ctx index c stores blocks 2c and 2c + 1 of each sequence.
All inputs are finite; a program needn't handle non-finite values.
Results may differ from a plain program's by a relative error of at most 0.02.
Values may be sent and summed in bfloat16 or wider, within the bound.
No kernel may reach another device: no remote copies, remote signals or barrier semaphores. Data moves between devices by JAX's collectives and lax.ppermute only.
A program may use at most 128 MiB of HBM per device.

v0:
```python
from functools import partial
import jax
import jax.numpy as jnp
from jax import lax
from jax.sharding import PartitionSpec as P

HD = 64
BLOCK = 128
THETA = 130000.0
EPS = 1e-05


def shifted(block, axis, distance):
    devices = range(lax.axis_size(axis))
    route = [((i - distance) % len(devices), i) for i in devices]
    return lax.ppermute(block, axis, route)


def rms_norm(hidden, gain):
    return hidden * lax.rsqrt(jnp.mean(hidden * hidden, axis=-1, keepdims=True) + EPS) * gain


def rotary(values, places):
    row_count = values.shape[0]
    by_heads = values.reshape(row_count, -1, HD)
    halfway = HD // 2
    inverse = THETA ** (-(jnp.arange(halfway, dtype=jnp.float32) * 2.0) / HD)
    angle = places.astype(jnp.float32)[:, None] * inverse[None, :]
    angle = jnp.concatenate([angle, angle], axis=1)
    cosine = jnp.cos(angle)[:, None, :]
    sine = jnp.sin(angle)[:, None, :]
    turned = jnp.concatenate([-by_heads[..., halfway:], by_heads[..., :halfway]], axis=-1)
    return (by_heads * cosine + turned * sine).reshape(row_count, -1)


def gated(gate, upward):
    return jax.nn.silu(gate) * upward


def product(left, right):
    return jnp.dot(left, right, preferred_element_type=jnp.float32)


def contract_rows(left, right):
    return lax.dot_general(
        left, right, (((0,), (0,)), ((), ())), preferred_element_type=jnp.float32
    )


def contract_cols(left, right):
    return lax.dot_general(
        left, right, (((1,), (1,)), ((), ())), preferred_element_type=jnp.float32
    )


def key_places(order, first_row, row_total):
    stored = first_row + jnp.arange(row_total, dtype=jnp.int32)
    group_slot = stored // BLOCK
    slot_table = jnp.arange(order.shape[0], dtype=jnp.int32)
    block_place = jnp.sum(
        jnp.where(group_slot[:, None] == slot_table[None, :], order[None, :], 0), axis=1
    )
    return block_place * BLOCK + stored % BLOCK


def exp_scores(query_heads, query_places, key_rows, key_pos):
    row_total = key_rows.shape[0]
    key_heads = key_rows.reshape(row_total, -1, HD)
    scores = (
        jnp.einsum("qhd,khd->hqk", query_heads, key_heads, preferred_element_type=jnp.float32)
        * 0.125
    )
    allowed = query_places[:, None] >= key_pos[None, :]
    return (jnp.where(allowed[None], jnp.exp(scores), 0.0), key_heads)


def per_device(
    tokens,
    query_weight,
    key_weight,
    value_weight,
    output_weight,
    gate_weight,
    up_weight,
    down_weight,
    attention_gain,
    feedforward_gain,
    order,
    cotangent,
):
    rows_local = tokens.shape[0]
    ctx_index = lax.axis_index("ctx")
    ctx_total = lax.axis_size("ctx")
    gathered = (
        lax.all_gather(query_weight, ("seq", "ctx"), axis=0, tiled=True),
        lax.all_gather(key_weight, ("seq", "ctx"), axis=0, tiled=True),
        lax.all_gather(value_weight, ("seq", "ctx"), axis=0, tiled=True),
        lax.all_gather(output_weight, ("seq", "ctx"), axis=1, tiled=True),
        lax.all_gather(gate_weight, ("seq", "ctx"), axis=0, tiled=True),
        lax.all_gather(up_weight, ("seq", "ctx"), axis=0, tiled=True),
        lax.all_gather(down_weight, ("seq", "ctx"), axis=1, tiled=True),
        lax.all_gather(attention_gain, ("seq", "ctx"), axis=0, tiled=True),
        lax.all_gather(feedforward_gain, ("seq", "ctx"), axis=0, tiled=True),
    )
    (
        full_query,
        full_key,
        full_value,
        full_output,
        full_gate,
        full_up,
        full_down,
        gain_first,
        gain_second,
    ) = gathered
    inputs = tokens.astype(jnp.float32)
    query_places = key_places(order, ctx_index * rows_local, rows_local)
    normed_value, norm_back_first = jax.vjp(rms_norm, inputs, gain_first.astype(jnp.float32))
    normed = normed_value.astype(jnp.bfloat16)
    rope_here = partial(rotary, places=query_places)
    query_rot, query_back = jax.vjp(rope_here, product(normed, full_query))
    key_rot, key_back = jax.vjp(rope_here, product(normed, full_key))
    value_rows = product(normed, full_value).astype(jnp.bfloat16)
    query_rows = query_rot.astype(jnp.bfloat16)
    key_rows = key_rot.astype(jnp.bfloat16)
    width = query_rows.shape[1]
    head_count = width // HD
    query_heads = query_rows.reshape(rows_local, head_count, HD)
    packed = jnp.stack([key_rows, value_rows])
    empty_totals = jnp.zeros((rows_local, head_count), jnp.float32)
    empty_numerator = jnp.zeros((rows_local, width), jnp.float32)
    arrived = lax.all_gather(packed, "ctx", axis=1, tiled=True)
    row_total = arrived.shape[1]

    def one_block(block_index, partial_state):
        first_row = block_index * rows_local
        section = lax.dynamic_slice_in_dim(arrived, first_row, rows_local, 1)
        key_pos = key_places(order, first_row, rows_local)
        weights, key_heads = exp_scores(query_heads, query_places, section[0], key_pos)
        value_heads = section[1].reshape(rows_local, -1, HD)
        totals, numerator = partial_state
        totals = totals + jnp.sum(weights, axis=2).T
        numerator = numerator + jnp.einsum(
            "hqk,khd->qhd",
            weights.astype(jnp.bfloat16),
            value_heads,
            preferred_element_type=jnp.float32,
        ).reshape(rows_local, width)
        return (totals, numerator)

    totals, numerator = lax.fori_loop(
        0, row_total // rows_local, one_block, (empty_totals, empty_numerator)
    )
    numerator_heads = numerator.reshape(rows_local, head_count, HD)
    mixed = (numerator_heads / totals[:, :, None]).astype(jnp.bfloat16).reshape(rows_local, width)
    middle = inputs + lax.psum(product(mixed, full_output), "tp")
    normed_two_value, norm_back_second = jax.vjp(rms_norm, middle, gain_second.astype(jnp.float32))
    normed_two = normed_two_value.astype(jnp.bfloat16)
    activated, gated_back = jax.vjp(
        gated, product(normed_two, full_gate), product(normed_two, full_up)
    )
    hidden = activated.astype(jnp.bfloat16)
    block_output = middle + lax.psum(product(hidden, full_down).astype(jnp.bfloat16), "tp").astype(
        jnp.float32
    )
    back_weights = (
        lax.all_gather(query_weight, ("seq", "ctx"), axis=0, tiled=True),
        lax.all_gather(key_weight, ("seq", "ctx"), axis=0, tiled=True),
        lax.all_gather(value_weight, ("seq", "ctx"), axis=0, tiled=True),
        lax.all_gather(output_weight, ("seq", "ctx"), axis=1, tiled=True),
        lax.all_gather(gate_weight, ("seq", "ctx"), axis=0, tiled=True),
        lax.all_gather(up_weight, ("seq", "ctx"), axis=0, tiled=True),
        lax.all_gather(down_weight, ("seq", "ctx"), axis=1, tiled=True),
        lax.all_gather(attention_gain, ("seq", "ctx"), axis=0, tiled=True),
        lax.all_gather(feedforward_gain, ("seq", "ctx"), axis=0, tiled=True),
    )
    (
        back_query,
        back_key,
        back_value,
        back_output,
        back_gate,
        back_up,
        back_down,
        gain_unused,
        gain_spare,
    ) = back_weights
    down_grad = contract_rows(hidden, cotangent)
    hidden_grad = contract_cols(cotangent, back_down)
    gate_grad, upward_grad = gated_back(hidden_grad)
    gate_grad = gate_grad.astype(jnp.bfloat16)
    upward_grad = upward_grad.astype(jnp.bfloat16)
    gate_wgrad = contract_rows(normed_two, gate_grad)
    upward_wgrad = contract_rows(normed_two, upward_grad)
    normed_two_grad = lax.psum(
        contract_cols(gate_grad, back_gate) + contract_cols(upward_grad, back_up), "tp"
    )
    middle_norm_grad, second_gain_grad = norm_back_second(normed_two_grad)
    middle_grad = cotangent.astype(jnp.float32) + middle_norm_grad
    branch_grad = middle_grad.astype(jnp.bfloat16)
    output_wgrad = contract_rows(mixed, branch_grad)
    mixed_grad = contract_cols(branch_grad, back_output).reshape(rows_local, head_count, HD)
    numerator_grad = (mixed_grad / totals[:, :, None]).astype(jnp.bfloat16)
    totals_grad = -jnp.sum(mixed_grad * numerator_heads, axis=2) / (totals * totals)
    totals_grad_heads = totals_grad.T[:, :, None]

    def visit(turn_index, state):
        visiting, carried, query_acc = state
        source = (ctx_index - turn_index) % ctx_total
        key_pos = key_places(order, source * rows_local, rows_local)
        weights, key_heads = exp_scores(query_heads, query_places, visiting[0], key_pos)
        value_heads = visiting[1].reshape(rows_local, -1, HD)
        through = jnp.einsum(
            "qhd,khd->hqk", numerator_grad, value_heads, preferred_element_type=jnp.float32
        )
        slopes = (weights * (through + totals_grad_heads)).astype(jnp.bfloat16)
        query_acc = (
            query_acc
            + jnp.einsum("hqk,khd->qhd", slopes, key_heads, preferred_element_type=jnp.float32)
            * 0.125
        )
        key_term = (
            jnp.einsum("hqk,qhd->khd", slopes, query_heads, preferred_element_type=jnp.float32)
            * 0.125
        )
        value_term = jnp.einsum(
            "hqk,qhd->khd",
            weights.astype(jnp.bfloat16),
            numerator_grad,
            preferred_element_type=jnp.float32,
        )
        carried = carried + jnp.stack(
            [key_term.reshape(rows_local, width), value_term.reshape(rows_local, width)]
        )
        visiting = shifted(visiting, "ctx", 1)
        carried = shifted(carried, "ctx", 1)
        return (visiting, carried, query_acc)

    start_state = (
        packed,
        jnp.zeros((2, rows_local, width), jnp.float32),
        jnp.zeros((rows_local, head_count, HD), jnp.float32),
    )
    ended, key_value_grad, query_acc = lax.fori_loop(0, ctx_total, visit, start_state)
    query_proj_grad = query_back(query_acc.reshape(rows_local, width))[0].astype(jnp.bfloat16)
    key_proj_grad = key_back(key_value_grad[0])[0].astype(jnp.bfloat16)
    value_grad = key_value_grad[1].astype(jnp.bfloat16)
    query_wgrad = contract_rows(normed, query_proj_grad)
    key_wgrad = contract_rows(normed, key_proj_grad)
    value_wgrad = contract_rows(normed, value_grad)
    normed_grad = lax.psum(
        (
            contract_cols(query_proj_grad, back_query)
            + contract_cols(key_proj_grad, back_key)
            + contract_cols(value_grad, back_value)
        ).astype(jnp.bfloat16),
        "tp",
    ).astype(jnp.float32)
    input_norm_grad, first_gain_grad = norm_back_first(normed_grad)
    input_grad = middle_grad + input_norm_grad
    scattered = (
        lax.psum_scatter(
            query_wgrad.astype(jnp.bfloat16), ("seq", "ctx"), scatter_dimension=0, tiled=True
        ).astype(jnp.float32),
        lax.psum_scatter(
            key_wgrad.astype(jnp.bfloat16), ("seq", "ctx"), scatter_dimension=0, tiled=True
        ).astype(jnp.float32),
        lax.psum_scatter(
            value_wgrad.astype(jnp.bfloat16), ("seq", "ctx"), scatter_dimension=0, tiled=True
        ).astype(jnp.float32),
        lax.psum_scatter(
            output_wgrad.astype(jnp.bfloat16), ("seq", "ctx"), scatter_dimension=1, tiled=True
        ).astype(jnp.float32),
        lax.psum_scatter(
            gate_wgrad.astype(jnp.bfloat16), ("seq", "ctx"), scatter_dimension=0, tiled=True
        ).astype(jnp.float32),
        lax.psum_scatter(
            upward_wgrad.astype(jnp.bfloat16), ("seq", "ctx"), scatter_dimension=0, tiled=True
        ).astype(jnp.float32),
        lax.psum_scatter(
            down_grad.astype(jnp.bfloat16), ("seq", "ctx"), scatter_dimension=1, tiled=True
        ).astype(jnp.float32),
        lax.psum_scatter(
            first_gain_grad.astype(jnp.bfloat16), ("seq", "ctx"), scatter_dimension=0, tiled=True
        ).astype(jnp.float32),
        lax.psum_scatter(
            second_gain_grad.astype(jnp.bfloat16), ("seq", "ctx"), scatter_dimension=0, tiled=True
        ).astype(jnp.float32),
    )
    return (
        block_output.astype(jnp.bfloat16),
        input_grad,
        scattered[0],
        scattered[1],
        scattered[2],
        scattered[3],
        scattered[4],
        scattered[5],
        scattered[6],
        scattered[7],
        scattered[8],
    )


def solution(mesh):
    placed = (
        P(("seq", "ctx"), None),
        P(("seq", "ctx"), "tp"),
        P(("seq", "ctx"), "tp"),
        P(("seq", "ctx"), "tp"),
        P("tp", ("seq", "ctx")),
        P(("seq", "ctx"), "tp"),
        P(("seq", "ctx"), "tp"),
        P("tp", ("seq", "ctx")),
        P(("seq", "ctx")),
        P(("seq", "ctx")),
        P(),
        P(("seq", "ctx"), None),
    )
    return jax.shard_map(
        per_device,
        mesh=mesh,
        in_specs=placed,
        out_specs=(
            P(("seq", "ctx"), None),
            P(("seq", "ctx"), None),
            P(("seq", "ctx"), "tp"),
            P(("seq", "ctx"), "tp"),
            P(("seq", "ctx"), "tp"),
            P("tp", ("seq", "ctx")),
            P(("seq", "ctx"), "tp"),
            P(("seq", "ctx"), "tp"),
            P("tp", ("seq", "ctx")),
            P(("seq", "ctx")),
            P(("seq", "ctx")),
        ),
        check_vma=False,
    )
```

profile of v0, /device:TPU:0, one launch (start us, length us, event | category | flops | bytes accessed | tf_op | source)
XLA Modules:
  0.0 1750.2 jit_solution(15163281541108414726)
XLA Ops:
  10.1 22.3 %all-gather = bf16[8,1,256]{2,1,0:T(2,128)(2,1)S(1)} all-gather(bf16[1,1,256]{2,1,0:T(2,128)(2,1)S(1)} %reshape.359), channel_id=1, replica_groups=mesh['seq'=2,'ctx'=4,'tp'=4] {'seq','ctx'}, dimensions={0}, use_global_device_ids=true | all-gather | bytes 4608 | tf_op jit(solution)/shard_map/all_gather | solution.py:102
  34.6 27.6 %all-gather.11.cloned.1.call-done = bf16[2048,512]{1,0:T(8,128)(2,1)} async-done(((bf16[256,512]{1,0:T(8,128)(2,1)}), bf16[2048,512]{1,0:T(8,128)(2,1)}) %all-gather.11.cloned.1.call-update) | async-done | bytes 2097168 | tf_op jit(solution)/shard_map/all_gather | solution.py:96
  64.7 47.4 %all-gather.17.cloned.1.call-done = bf16[2048,512]{1,0:T(8,128)(2,1)} async-done(((bf16[256,512]{1,0:T(8,128)(2,1)}), bf16[2048,512]{1,0:T(8,128)(2,1)}) %all-gather.17.cloned.1.call-update) | async-done | bytes 2097168 | tf_op jit(solution)/shard_map/all_gather | solution.py:95
  123.1 39.0 %all-gather.13.cloned.1.call-done = bf16[2048,512]{1,0:T(8,128)(2,1)} async-done(((bf16[256,512]{1,0:T(8,128)(2,1)}), bf16[2048,512]{1,0:T(8,128)(2,1)}) %all-gather.13.cloned.1.call-update) | async-done | bytes 2097168 | tf_op jit(solution)/shard_map/all_gather | solution.py:97
  166.1 43.8 %all-gather.15.cloned.1.call-done = bf16[2,1024,512]{2,1,0:T(8,128)(2,1)} async-done(((bf16[2,256,512]{2,1,0:T(8,128)(2,1)}), bf16[2,1024,512]{2,1,0:T(8,128)(2,1)}) %all-gather.15.cloned.1.call-update) | async-done | bytes 2097168 | tf_op jit(solution)/shard_map/all_gather | solution.py:132
  209.9 22.9 %while.39 = (s32[]{:T(128)}, f32[256,8]{0,1:T(8,128)S(1)}, f32[256,512]{0,1:T(8,128)}, s32[256]{0:T(256)}, s32[8]{0:T(128)}, /*index=5*/bf16[2,1024,512]{2,1,0:T...) while((s32[]{:T(128)}, f32[256,8]{0,1:T(8,128)S(1)}, ...), condition=%wide.region_5.6_spmd.clone, body=%wide.region_2.5_spmd.clone.sunk | while | flops 137706752 | bytes 9411818 | solution.py:151
  233.8 27.7 %all-gather.19.cloned.1.call-done = bf16[512,2048]{1,0:T(8,128)(2,1)} async-done(((bf16[512,256]{1,0:T(8,128)(2,1)}), bf16[512,2048]{1,0:T(8,128)(2,1)}) %all-gather.19.cloned.1.call-update) | async-done | bytes 2097168 | tf_op jit(solution)/shard_map/all_gather | solution.py:98
  286.3 28.6 %all-reduce.12.cloned.1.call-done = f32[256,2048]{1,0:T(8,128)} async-done(((f32[256,2048]{1,0:T(8,128)}), f32[256,2048]{1,0:T(8,128)}) %all-reduce.12.cloned.1.call-update) | async-done | bytes 2097168 | tf_op jit(solution)/shard_map/psum | solution.py:156
  317.8 124.5 %all-gather.21.cloned.1.call-done = bf16[2048,2048]{1,0:T(8,128)(2,1)} async-done(((bf16[256,2048]{1,0:T(8,128)(2,1)}), bf16[2048,2048]{1,0:T(8,128)(2,1)}) %all-gather.21.cloned.1.call-update) | async-done | bytes 8388624 | tf_op jit(solution)/shard_map/all_gather | solution.py:99
  449.3 118.5 %all-gather.23.cloned.1.call-done = bf16[2048,2048]{1,0:T(8,128)(2,1)} async-done(((bf16[256,2048]{1,0:T(8,128)(2,1)}), bf16[2048,2048]{1,0:T(8,128)(2,1)}) %all-gather.23.cloned.1.call-update) | async-done | bytes 8388624 | tf_op jit(solution)/shard_map/all_gather | solution.py:100
  574.8 118.8 %all-gather.25.cloned.1.call-done = bf16[2048,2048]{1,0:T(8,128)(2,1)} async-done(((bf16[2048,256]{1,0:T(8,128)(2,1)}), bf16[2048,2048]{1,0:T(8,128)(2,1)}) %all-gather.25.cloned.1.call-update) | async-done | bytes 8388624 | tf_op jit(solution)/shard_map/all_gather | solution.py:101
  722.4 40.2 %all-reduce.14.cloned.1.call-done = f32[256,2048]{1,0:T(8,128)} async-done(((f32[256,2048]{1,0:T(8,128)}), f32[256,2048]{1,0:T(8,128)}) %all-reduce.14.cloned.1.call-update) | async-done | bytes 2097168 | tf_op jit(solution)/shard_map/psum | solution.py:195
  768.8 173.2 %while.40 = (s32[]{:T(128)}, bf16[2,256,512]{1,2,0:T(8,128)(2,1)}, f32[2,256,512]{1,2,0:T(8,128)S(1)}, f32[256,8,64]{0,2,1:T(8,128)}, s32[256]{0:T(256)}, /*inde...) while((s32[]{:T(128)}, bf16[2,256,512]{1,2,0:T(8,128)(2,1)}, ...), condition=%wide.region_14.15_spmd.clone, body=%wide.region_12.14_spmd.clone.sunk | while | flops 340866304 | bytes 25116048 | solution.py:244
  779.5 34.0 %collective-permute-done = bf16[2,256,512]{1,2,0:T(8,128)(2,1)} collective-permute-done((bf16[2,256,512]{1,2,0:T(8,128)(2,1)S(1)}, bf16[2,256,512]{1,2,0:T(8,128)(2,1)}, u32[]{:S(2)}, u32[]{:S(2)}) %collective-permute-start) | collective-permute-done | bytes 524320 | tf_op jit(solution)/shard_map/while/body/eval_jaxpr/ppermute | solution.py:16
  823.4 33.8 %collective-permute-done = bf16[2,256,512]{1,2,0:T(8,128)(2,1)} collective-permute-done((bf16[2,256,512]{1,2,0:T(8,128)(2,1)S(1)}, bf16[2,256,512]{1,2,0:T(8,128)(2,1)}, u32[]{:S(2)}, u32[]{:S(2)}) %collective-permute-start) | collective-permute-done | bytes 524320 | tf_op jit(solution)/shard_map/while/body/eval_jaxpr/ppermute | solution.py:16
  866.0 34.1 %collective-permute-done = bf16[2,256,512]{1,2,0:T(8,128)(2,1)} collective-permute-done((bf16[2,256,512]{1,2,0:T(8,128)(2,1)S(1)}, bf16[2,256,512]{1,2,0:T(8,128)(2,1)}, u32[]{:S(2)}, u32[]{:S(2)}) %collective-permute-start) | collective-permute-done | bytes 524320 | tf_op jit(solution)/shard_map/while/body/eval_jaxpr/ppermute | solution.py:16
  908.9 33.2 %collective-permute-done = bf16[2,256,512]{1,2,0:T(8,128)(2,1)} collective-permute-done((bf16[2,256,512]{1,2,0:T(8,128)(2,1)S(1)}, bf16[2,256,512]{1,2,0:T(8,128)(2,1)}, u32[]{:S(2)}, u32[]{:S(2)}) %collective-permute-start) | collective-permute-done | bytes 524320 | tf_op jit(solution)/shard_map/while/body/eval_jaxpr/ppermute | solution.py:16
  1029.8 42.1 %reduce-scatter.14.cloned.1.call-done = bf16[512,256]{1,0:T(8,128)(2,1)} async-done(((bf16[512,2048]{1,0:T(8,128)(2,1)}), bf16[512,256]{1,0:T(8,128)(2,1)}) %reduce-scatter.14.cloned.1.call-update) | async-done | bytes 262160 | tf_op jit(solution)/shard_map/reduce_scatter | solution.py:271
  1073.7 69.6 %reduce-scatter.8.cloned.1.call-done = bf16[256,512]{1,0:T(8,128)(2,1)} async-done(((bf16[2048,512]{1,0:T(8,128)(2,1)}), bf16[256,512]{1,0:T(8,128)(2,1)}) %reduce-scatter.8.cloned.1.call-update) | async-done | bytes 262160 | tf_op jit(solution)/shard_map/reduce_scatter | solution.py:262
  1145.1 68.9 %reduce-scatter.10.cloned.1.call-done = bf16[256,512]{1,0:T(8,128)(2,1)} async-done(((bf16[2048,512]{1,0:T(8,128)(2,1)}), bf16[256,512]{1,0:T(8,128)(2,1)}) %reduce-scatter.10.cloned.1.call-update) | async-done | bytes 262160 | tf_op jit(solution)/shard_map/reduce_scatter | solution.py:265
  1215.7 68.9 %reduce-scatter.12.cloned.1.call-done = bf16[256,512]{1,0:T(8,128)(2,1)} async-done(((bf16[2048,512]{1,0:T(8,128)(2,1)}), bf16[256,512]{1,0:T(8,128)(2,1)}) %reduce-scatter.12.cloned.1.call-update) | async-done | bytes 262160 | tf_op jit(solution)/shard_map/reduce_scatter | solution.py:268
  1286.4 150.1 %reduce-scatter.16.cloned.1.call-done = bf16[256,2048]{1,0:T(8,128)(2,1)} async-done(((bf16[2048,2048]{1,0:T(8,128)(2,1)}), bf16[256,2048]{1,0:T(8,128)(2,1)}) %reduce-scatter.16.cloned.1.call-update) | async-done | bytes 1048592 | tf_op jit(solution)/shard_map/reduce_scatter | solution.py:274
  1439.3 148.7 %reduce-scatter.18.cloned.1.call-done = bf16[256,2048]{1,0:T(8,128)(2,1)} async-done(((bf16[2048,2048]{1,0:T(8,128)(2,1)}), bf16[256,2048]{1,0:T(8,128)(2,1)}) %reduce-scatter.18.cloned.1.call-update) | async-done | bytes 1048592 | tf_op jit(solution)/shard_map/reduce_scatter | solution.py:277
  1590.8 149.6 %reduce-scatter.20.cloned.1.call-done = bf16[2048,256]{1,0:T(8,128)(2,1)} async-done(((bf16[2048,2048]{1,0:T(8,128)(2,1)}), bf16[2048,256]{1,0:T(8,128)(2,1)}) %reduce-scatter.20.cloned.1.call-update) | async-done | bytes 1048592 | tf_op jit(solution)/shard_map/reduce_scatter | solution.py:280
  (304 shorter events, 262.7 us)
Async XLA Ops:
  7.2 55.0 %all-gather.11.cloned.1.call-start = ((), (), s32[]{:S(2)}) async-start(), calls=%async_computation.7 | async-start | bytes 2359296 | tf_op jit(solution)/shard_map/all_gather | solution.py:96
  7.9 104.2 %all-gather.17.cloned.1.call-start = ((), (), s32[]{:S(2)}) async-start(), calls=%async_computation.10 | async-start | bytes 2359296 | tf_op jit(solution)/shard_map/all_gather | solution.py:95
  8.7 153.4 %all-gather.13.cloned.1.call-start = ((), (), s32[]{:S(2)}) async-start(), calls=%async_computation.8 | async-start | bytes 2359296 | tf_op jit(solution)/shard_map/all_gather | solution.py:97
  9.4 200.5 %all-gather.15.cloned.1.call-start = ((), (), s32[]{:S(2)}) async-start(), calls=%async_computation.9 | async-start | bytes 2621440 | tf_op jit(solution)/shard_map/all_gather | solution.py:132
  165.3 96.2 %all-gather.19.cloned.1.call-start = ((), (), s32[]{:S(2)}) async-start(), calls=%async_computation.11 | async-start | bytes 2359296 | tf_op jit(solution)/shard_map/all_gather | solution.py:98
  165.9 149.0 %all-reduce.12.cloned.1.call-start = ((), (), s32[]{:S(2)}) async-start(), calls=%async_computation.12 | async-start | bytes 4194304 | tf_op jit(solution)/shard_map/psum | solution.py:156
  265.2 177.1 %all-gather.21.cloned.1.call-start = ((), (), s32[]{:S(2)}) async-start(), calls=%async_computation.13 | async-start | bytes 9437184 | tf_op jit(solution)/shard_map/all_gather | solution.py:99
  266.0 301.8 %all-gather.23.cloned.1.call-start = ((), (), s32[]{:S(2)}) async-start(), calls=%async_computation.14 | async-start | bytes 9437184 | tf_op jit(solution)/shard_map/all_gather | solution.py:100
  266.7 426.9 %all-gather.25.cloned.1.call-start = ((), (), s32[]{:S(2)}) async-start(), calls=%async_computation.15 | async-start | bytes 9437184 | tf_op jit(solution)/shard_map/all_gather | solution.py:101
  267.5 495.2 %all-reduce.14.cloned.1.call-start = ((), (), s32[]{:S(2)}) async-start(), calls=%async_computation.16 | async-start | bytes 4194304 | tf_op jit(solution)/shard_map/psum | solution.py:195
  712.9 286.6 %all-reduce.16.cloned.1.call-start = ((), (), s32[]{:S(2)}) async-start(), calls=%async_computation.24 | async-start | bytes 4194304 | tf_op jit(solution)/shard_map/psum | solution.py:163
  775.3 38.2 %collective-permute-start.1 = (f32[2,256,512]{1,2,0:T(8,128)}, f32[2,256,512]{1,2,0:T(8,128)S(1)}, u32[]{:S(2)}, u32[]{:S(2)}) collective-permute-start(f32[2,256,512]{1,2,0:T(8,128)} %maximum_add_fusion.2), channel_id=1, source_target_pairs={{12,0},{0,4},{4,8},{8,12},{13,1},{1,5},{5,9},{9,13},{14,2},{2,6},{... | collective-permute-start | bytes 3145736 | tf_op jit(solution)/shard_map/while/body/eval_jaxpr/ppermute | solution.py:16
  776.8 36.7 %collective-permute-start = (bf16[2,256,512]{1,2,0:T(8,128)(2,1)S(1)}, bf16[2,256,512]{1,2,0:T(8,128)(2,1)}, u32[]{:S(2)}, u32[]{:S(2)}) collective-permute-start(bf16[2,256,512]{1,2,0:T(8,128)(2,1)S(1)} %copy.95), channel_id=1, source_target_pairs={{12,0},{0,4},{4,8},{8,12},{13,1},{1,5},{5,9},{9,13},{14,2},{2,6},{... | collective-permute-start | bytes 1572872 | tf_op jit(solution)/shard_map/while/body/eval_jaxpr/ppermute | solution.py:16
  820.0 37.3 %collective-permute-start.1 = (f32[2,256,512]{1,2,0:T(8,128)}, f32[2,256,512]{1,2,0:T(8,128)S(1)}, u32[]{:S(2)}, u32[]{:S(2)}) collective-permute-start(f32[2,256,512]{1,2,0:T(8,128)} %maximum_add_fusion.2), channel_id=1, source_target_pairs={{12,0},{0,4},{4,8},{8,12},{13,1},{1,5},{5,9},{9,13},{14,2},{2,6},{... | collective-permute-start | bytes 3145736 | tf_op jit(solution)/shard_map/while/body/eval_jaxpr/ppermute | solution.py:16
  820.0 37.3 %collective-permute-start = (bf16[2,256,512]{1,2,0:T(8,128)(2,1)S(1)}, bf16[2,256,512]{1,2,0:T(8,128)(2,1)}, u32[]{:S(2)}, u32[]{:S(2)}) collective-permute-start(bf16[2,256,512]{1,2,0:T(8,128)(2,1)S(1)} %copy.95), channel_id=1, source_target_pairs={{12,0},{0,4},{4,8},{8,12},{13,1},{1,5},{5,9},{9,13},{14,2},{2,6},{... | collective-permute-start | bytes 1572872 | tf_op jit(solution)/shard_map/while/body/eval_jaxpr/ppermute | solution.py:16
  863.8 36.4 %collective-permute-start.1 = (f32[2,256,512]{1,2,0:T(8,128)}, f32[2,256,512]{1,2,0:T(8,128)S(1)}, u32[]{:S(2)}, u32[]{:S(2)}) collective-permute-start(f32[2,256,512]{1,2,0:T(8,128)} %maximum_add_fusion.2), channel_id=1, source_target_pairs={{12,0},{0,4},{4,8},{8,12},{13,1},{1,5},{5,9},{9,13},{14,2},{2,6},{... | collective-permute-start | bytes 3145736 | tf_op jit(solution)/shard_map/while/body/eval_jaxpr/ppermute | solution.py:16
  863.8 36.4 %collective-permute-start = (bf16[2,256,512]{1,2,0:T(8,128)(2,1)S(1)}, bf16[2,256,512]{1,2,0:T(8,128)(2,1)}, u32[]{:S(2)}, u32[]{:S(2)}) collective-permute-start(bf16[2,256,512]{1,2,0:T(8,128)(2,1)S(1)} %copy.95), channel_id=1, source_target_pairs={{12,0},{0,4},{4,8},{8,12},{13,1},{1,5},{5,9},{9,13},{14,2},{2,6},{... | collective-permute-start | bytes 1572872 | tf_op jit(solution)/shard_map/while/body/eval_jaxpr/ppermute | solution.py:16
  949.9 122.0 %reduce-scatter.14.cloned.1.call-start = ((), (), s32[]{:S(2)}) async-start(), calls=%async_computation.20 | async-start | bytes 2359296 | tf_op jit(solution)/shard_map/reduce_scatter | solution.py:271
  954.5 188.8 %reduce-scatter.8.cloned.1.call-start = ((), (), s32[]{:S(2)}) async-start(), calls=%async_computation.17 | async-start | bytes 2359296 | tf_op jit(solution)/shard_map/reduce_scatter | solution.py:262
  957.9 256.0 %reduce-scatter.10.cloned.1.call-start = ((), (), s32[]{:S(2)}) async-start(), calls=%async_computation.18 | async-start | bytes 2359296 | tf_op jit(solution)/shard_map/reduce_scatter | solution.py:265
  960.3 324.3 %reduce-scatter.12.cloned.1.call-start = ((), (), s32[]{:S(2)}) async-start(), calls=%async_computation.19 | async-start | bytes 2359296 | tf_op jit(solution)/shard_map/reduce_scatter | solution.py:268
  962.7 473.8 %reduce-scatter.16.cloned.1.call-start = ((), (), s32[]{:S(2)}) async-start(), calls=%async_computation.21 | async-start | bytes 9437184 | tf_op jit(solution)/shard_map/reduce_scatter | solution.py:274
  969.6 618.4 %reduce-scatter.18.cloned.1.call-start = ((), (), s32[]{:S(2)}) async-start(), calls=%async_computation.22 | async-start | bytes 9437184 | tf_op jit(solution)/shard_map/reduce_scatter | solution.py:277
  976.5 763.9 %reduce-scatter.20.cloned.1.call-start = ((), (), s32[]{:S(2)}) async-start(), calls=%async_computation.23 | async-start | bytes 9437184 | tf_op jit(solution)/shard_map/reduce_scatter | solution.py:280
  (44 other events, 1377.5 us)
Sparse Core Ops, SparseCore 0:
  10.1 52.0 all-gather.10
  64.3 47.7 all-gather.16
  114.3 47.7 all-gather.12
  165.4 44.4 all-gather.14
  211.7 49.7 all-gather.18
  265.3 49.5 all-reduce.11
  317.3 125.0 all-gather.20
  444.7 123.1 all-gather.22
  570.0 123.5 all-gather.24
  713.0 49.5 all-reduce.13
  950.0 49.4 all-reduce.15
  1003.4 68.4 reduce-scatter.13
  1076.4 66.8 reduce-scatter.7
  1147.1 66.8 reduce-scatter.9
  1217.7 66.8 reduce-scatter.11
  1288.5 147.9 reduce-scatter.15
  1440.0 147.9 reduce-scatter.17
  1592.0 148.4 reduce-scatter.19
where the time goes:
time: 1760 us; the launch traced here: 1750 us
  waiting for transfers between devices  1470 us (84%)
  matrix products  106 us (6%)
  other arithmetic  63.6 us (4%)
  blocking collectives  62.5 us (4%)
  local copies, waits for them, and re-layouts  28.8 us (2%)
    reduce_scatter x1, waiting for transfers between devices, per_device(): lax.psum_scatter(gate_wgrad.astype(jnp.bfloat16), ('seq', 'ctx'), scatter...  150 us
    reduce_scatter x1, waiting for transfers between devices, per_device(): lax.psum_scatter(down_grad.astype(jnp.bfloat16), ('seq', 'ctx'), scatter_...  150 us
    reduce_scatter x1, waiting for transfers between devices, per_device(): lax.psum_scatter(upward_wgrad.astype(jnp.bfloat16), ('seq', 'ctx'), scatt...  149 us
    ppermute x8, waiting for transfers between devices, shifted(): return lax.ppermute(block, axis, route)  135 us
    all_gather x1, waiting for transfers between devices, per_device(): lax.all_gather(gate_weight, ('seq', 'ctx'), axis=0, tiled=True)  125 us
    all_gather x1, waiting for transfers between devices, per_device(): lax.all_gather(down_weight, ('seq', 'ctx'), axis=1, tiled=True)  119 us
    all_gather x1, waiting for transfers between devices, per_device(): lax.all_gather(up_weight, ('seq', 'ctx'), axis=0, tiled=True)  118 us
    reduce_scatter x1, waiting for transfers between devices, per_device(): lax.psum_scatter(query_wgrad.astype(jnp.bfloat16), ('seq', 'ctx'), scatte...  69.6 us
  transfers between devices with their start and end apart: 26, of which 22 were waited for; matrix products, arithmetic and copies ran while one was open for 7% of the time, Pallas kernels for 0%

commit v1 on v0

--- a/solution.py
+++ b/solution.py
@@ -192,8 +192,11 @@
     upward_grad = upward_grad.astype(jnp.bfloat16)
     gate_wgrad = contract_rows(normed_two, gate_grad)
     upward_wgrad = contract_rows(normed_two, upward_grad)
-    normed_two_grad = lax.psum(
-        contract_cols(gate_grad, back_gate) + contract_cols(upward_grad, back_up), "tp"
+    normed_two_grad = jnp.sum(
+        lax.all_gather(
+            contract_cols(gate_grad, back_gate) + contract_cols(upward_grad, back_up), "tp"
+        ),
+        axis=0,
     )
     middle_norm_grad, second_gain_grad = norm_back_second(normed_two_grad)
     middle_grad = cotangent.astype(jnp.float32) + middle_norm_grad

time: 1760 us -> 1770 us (level)
    all_gather x0 -> x1, waiting for transfers between devices: none -> 46.9 us  [per_device(): lax.all_gather(contract_cols(gate_grad, back_gate) + contract_cols(upward...]
    psum x1 -> x0, waiting for transfers between devices: 40.2 us -> none  [per_device(): lax.psum(contract_cols(gate_grad, back_gate) + contract_cols(upward_grad,...]
where the time goes in v1:
time: 1770 us; the launch traced here: 1760 us
  waiting for transfers between devices  1470 us (83%)
  matrix products  106 us (6%)
  other arithmetic  69.3 us (4%)
  blocking collectives  62.6 us (4%)
  local copies, waits for them, and re-layouts  28.9 us (2%)
    reduce_scatter x1, waiting for transfers between devices, per_device(): lax.psum_scatter(gate_wgrad.astype(jnp.bfloat16), ('seq', 'ctx'), scatter...  150 us
    reduce_scatter x1, waiting for transfers between devices, per_device(): lax.psum_scatter(upward_wgrad.astype(jnp.bfloat16), ('seq', 'ctx'), scatt...  149 us
    reduce_scatter x1, waiting for transfers between devices, per_device(): lax.psum_scatter(down_grad.astype(jnp.bfloat16), ('seq', 'ctx'), scatter_...  149 us
    ppermute x8, waiting for transfers between devices, shifted(): return lax.ppermute(block, axis, route)  137 us
    all_gather x1, waiting for transfers between devices, per_device(): lax.all_gather(gate_weight, ('seq', 'ctx'), axis=0, tiled=True)  125 us
    all_gather x1, waiting for transfers between devices, per_device(): lax.all_gather(down_weight, ('seq', 'ctx'), axis=1, tiled=True)  119 us
    all_gather x1, waiting for transfers between devices, per_device(): lax.all_gather(up_weight, ('seq', 'ctx'), axis=0, tiled=True)  118 us
    reduce_scatter x1, waiting for transfers between devices, per_device(): lax.psum_scatter(query_wgrad.astype(jnp.bfloat16), ('seq', 'ctx'), scatte...  69 us
  transfers between devices with their start and end apart: 26, of which 22 were waited for; matrix products, arithmetic and copies ran while one was open for 7% of the time, Pallas kernels for 0%

profile of v1, /device:TPU:0, one launch (start us, length us, event | category | flops | bytes accessed | tf_op | source)
XLA Modules:
  0.0 1761.8 jit_solution(14619162004016420345)
XLA Ops:
  10.1 22.3 %all-gather.1 = bf16[8,1,256]{2,1,0:T(2,128)(2,1)S(1)} all-gather(bf16[1,1,256]{2,1,0:T(2,128)(2,1)S(1)} %reshape.360), channel_id=1, replica_groups=mesh['seq'=2,'ctx'=4,'tp'=4] {'seq','ctx'}, dimensions={0}, use_global_device_ids=true | all-gather | bytes 4608 | tf_op jit(solution)/shard_map/all_gather | solution.py:102
  34.6 27.6 %all-gather.13.cloned.1.call-done = bf16[2048,512]{1,0:T(8,128)(2,1)} async-done(((bf16[256,512]{1,0:T(8,128)(2,1)}), bf16[2048,512]{1,0:T(8,128)(2,1)}) %all-gather.13.cloned.1.call-update) | async-done | bytes 2097168 | tf_op jit(solution)/shard_map/all_gather | solution.py:96
  64.7 47.4 %all-gather.19.cloned.1.call-done = bf16[2048,512]{1,0:T(8,128)(2,1)} async-done(((bf16[256,512]{1,0:T(8,128)(2,1)}), bf16[2048,512]{1,0:T(8,128)(2,1)}) %all-gather.19.cloned.1.call-update) | async-done | bytes 2097168 | tf_op jit(solution)/shard_map/all_gather | solution.py:95
  123.1 39.0 %all-gather.15.cloned.1.call-done = bf16[2048,512]{1,0:T(8,128)(2,1)} async-done(((bf16[256,512]{1,0:T(8,128)(2,1)}), bf16[2048,512]{1,0:T(8,128)(2,1)}) %all-gather.15.cloned.1.call-update) | async-done | bytes 2097168 | tf_op jit(solution)/shard_map/all_gather | solution.py:97
  166.1 43.8 %all-gather.17.cloned.1.call-done = bf16[2,1024,512]{2,1,0:T(8,128)(2,1)} async-done(((bf16[2,256,512]{2,1,0:T(8,128)(2,1)}), bf16[2,1024,512]{2,1,0:T(8,128)(2,1)}) %all-gather.17.cloned.1.call-update) | async-done | bytes 2097168 | tf_op jit(solution)/shard_map/all_gather | solution.py:132
  209.9 22.9 %while.39 = (s32[]{:T(128)}, f32[256,8]{0,1:T(8,128)S(1)}, f32[256,512]{0,1:T(8,128)}, s32[256]{0:T(256)}, s32[8]{0:T(128)}, /*index=5*/bf16[2,1024,512]{2,1,0:T...) while((s32[]{:T(128)}, f32[256,8]{0,1:T(8,128)S(1)}, ...), condition=%wide.region_5.6_spmd.clone, body=%wide.region_2.5_spmd.clone.sunk | while | flops 137706752 | bytes 9411818 | solution.py:151
  233.8 27.7 %all-gather.21.cloned.1.call-done = bf16[512,2048]{1,0:T(8,128)(2,1)} async-done(((bf16[512,256]{1,0:T(8,128)(2,1)}), bf16[512,2048]{1,0:T(8,128)(2,1)}) %all-gather.21.cloned.1.call-update) | async-done | bytes 2097168 | tf_op jit(solution)/shard_map/all_gather | solution.py:98
  286.3 28.6 %all-reduce.11.cloned.1.call-done = f32[256,2048]{1,0:T(8,128)} async-done(((f32[256,2048]{1,0:T(8,128)}), f32[256,2048]{1,0:T(8,128)}) %all-reduce.11.cloned.1.call-update) | async-done | bytes 2097168 | tf_op jit(solution)/shard_map/psum | solution.py:156
  317.8 124.5 %all-gather.23.cloned.1.call-done = bf16[2048,2048]{1,0:T(8,128)(2,1)} async-done(((bf16[256,2048]{1,0:T(8,128)(2,1)}), bf16[2048,2048]{1,0:T(8,128)(2,1)}) %all-gather.23.cloned.1.call-update) | async-done | bytes 8388624 | tf_op jit(solution)/shard_map/all_gather | solution.py:99
  449.3 118.5 %all-gather.25.cloned.1.call-done = bf16[2048,2048]{1,0:T(8,128)(2,1)} async-done(((bf16[256,2048]{1,0:T(8,128)(2,1)}), bf16[2048,2048]{1,0:T(8,128)(2,1)}) %all-gather.25.cloned.1.call-update) | async-done | bytes 8388624 | tf_op jit(solution)/shard_map/all_gather | solution.py:100
  574.8 118.8 %all-gather.27.cloned.1.call-done = bf16[2048,2048]{1,0:T(8,128)(2,1)} async-done(((bf16[2048,256]{1,0:T(8,128)(2,1)}), bf16[2048,2048]{1,0:T(8,128)(2,1)}) %all-gather.27.cloned.1.call-update) | async-done | bytes 8388624 | tf_op jit(solution)/shard_map/all_gather | solution.py:101
  722.6 46.9 %all-gather.29.cloned.1.call-done = f32[1024,2048]{1,0:T(8,128)} async-done(((f32[256,2048]{1,0:T(8,128)}), f32[1024,2048]{1,0:T(8,128)}) %all-gather.29.cloned.1.call-update) | async-done | bytes 8388624 | tf_op jit(solution)/shard_map/all_gather | solution.py:196
  781.5 175.3 %while.40 = (s32[]{:T(128)}, bf16[2,256,512]{1,2,0:T(8,128)(2,1)}, f32[2,256,512]{1,2,0:T(8,128)S(1)}, f32[256,8,64]{0,2,1:T(8,128)}, s32[256]{0:T(256)}, /*inde...) while((s32[]{:T(128)}, bf16[2,256,512]{1,2,0:T(8,128)(2,1)}, ...), condition=%wide.region_14.15_spmd.clone, body=%wide.region_12.14_spmd.clone.sunk | while | flops 340866304 | bytes 25116048 | solution.py:247
  792.2 34.5 %collective-permute-done = bf16[2,256,512]{1,2,0:T(8,128)(2,1)} collective-permute-done((bf16[2,256,512]{1,2,0:T(8,128)(2,1)S(1)}, bf16[2,256,512]{1,2,0:T(8,128)(2,1)}, u32[]{:S(2)}, u32[]{:S(2)}) %collective-permute-start) | collective-permute-done | bytes 524320 | tf_op jit(solution)/shard_map/while/body/eval_jaxpr/ppermute | solution.py:16
  836.6 34.4 %collective-permute-done = bf16[2,256,512]{1,2,0:T(8,128)(2,1)} collective-permute-done((bf16[2,256,512]{1,2,0:T(8,128)(2,1)S(1)}, bf16[2,256,512]{1,2,0:T(8,128)(2,1)}, u32[]{:S(2)}, u32[]{:S(2)}) %collective-permute-start) | collective-permute-done | bytes 524320 | tf_op jit(solution)/shard_map/while/body/eval_jaxpr/ppermute | solution.py:16
  879.7 34.6 %collective-permute-done = bf16[2,256,512]{1,2,0:T(8,128)(2,1)} collective-permute-done((bf16[2,256,512]{1,2,0:T(8,128)(2,1)S(1)}, bf16[2,256,512]{1,2,0:T(8,128)(2,1)}, u32[]{:S(2)}, u32[]{:S(2)}) %collective-permute-start) | collective-permute-done | bytes 524320 | tf_op jit(solution)/shard_map/while/body/eval_jaxpr/ppermute | solution.py:16
  923.1 33.7 %collective-permute-done = bf16[2,256,512]{1,2,0:T(8,128)(2,1)} collective-permute-done((bf16[2,256,512]{1,2,0:T(8,128)(2,1)S(1)}, bf16[2,256,512]{1,2,0:T(8,128)(2,1)}, u32[]{:S(2)}, u32[]{:S(2)}) %collective-permute-start) | collective-permute-done | bytes 524320 | tf_op jit(solution)/shard_map/while/body/eval_jaxpr/ppermute | solution.py:16
  1044.0 41.4 %reduce-scatter.14.cloned.1.call-done = bf16[512,256]{1,0:T(8,128)(2,1)} async-done(((bf16[512,2048]{1,0:T(8,128)(2,1)}), bf16[512,256]{1,0:T(8,128)(2,1)}) %reduce-scatter.14.cloned.1.call-update) | async-done | bytes 262160 | tf_op jit(solution)/shard_map/reduce_scatter | solution.py:274
  1087.2 69.0 %reduce-scatter.8.cloned.1.call-done = bf16[256,512]{1,0:T(8,128)(2,1)} async-done(((bf16[2048,512]{1,0:T(8,128)(2,1)}), bf16[256,512]{1,0:T(8,128)(2,1)}) %reduce-scatter.8.cloned.1.call-update) | async-done | bytes 262160 | tf_op jit(solution)/shard_map/reduce_scatter | solution.py:265
  1157.9 68.4 %reduce-scatter.10.cloned.1.call-done = bf16[256,512]{1,0:T(8,128)(2,1)} async-done(((bf16[2048,512]{1,0:T(8,128)(2,1)}), bf16[256,512]{1,0:T(8,128)(2,1)}) %reduce-scatter.10.cloned.1.call-update) | async-done | bytes 262160 | tf_op jit(solution)/shard_map/reduce_scatter | solution.py:268
  1228.2 68.4 %reduce-scatter.12.cloned.1.call-done = bf16[256,512]{1,0:T(8,128)(2,1)} async-done(((bf16[2048,512]{1,0:T(8,128)(2,1)}), bf16[256,512]{1,0:T(8,128)(2,1)}) %reduce-scatter.12.cloned.1.call-update) | async-done | bytes 262160 | tf_op jit(solution)/shard_map/reduce_scatter | solution.py:271
  1298.3 149.7 %reduce-scatter.16.cloned.1.call-done = bf16[256,2048]{1,0:T(8,128)(2,1)} async-done(((bf16[2048,2048]{1,0:T(8,128)(2,1)}), bf16[256,2048]{1,0:T(8,128)(2,1)}) %reduce-scatter.16.cloned.1.call-update) | async-done | bytes 1048592 | tf_op jit(solution)/shard_map/reduce_scatter | solution.py:277
  1450.9 149.2 %reduce-scatter.18.cloned.1.call-done = bf16[256,2048]{1,0:T(8,128)(2,1)} async-done(((bf16[2048,2048]{1,0:T(8,128)(2,1)}), bf16[256,2048]{1,0:T(8,128)(2,1)}) %reduce-scatter.18.cloned.1.call-update) | async-done | bytes 1048592 | tf_op jit(solution)/shard_map/reduce_scatter | solution.py:280
  1602.8 149.1 %reduce-scatter.20.cloned.1.call-done = bf16[2048,256]{1,0:T(8,128)(2,1)} async-done(((bf16[2048,2048]{1,0:T(8,128)(2,1)}), bf16[2048,256]{1,0:T(8,128)(2,1)}) %reduce-scatter.20.cloned.1.call-update) | async-done | bytes 1048592 | tf_op jit(solution)/shard_map/reduce_scatter | solution.py:283
  (305 shorter events, 268.1 us)
Async XLA Ops:
  7.2 55.0 %all-gather.13.cloned.1.call-start = ((), (), s32[]{:S(2)}) async-start(), calls=%async_computation.7 | async-start | bytes 2359296 | tf_op jit(solution)/shard_map/all_gather | solution.py:96
  7.9 104.2 %all-gather.19.cloned.1.call-start = ((), (), s32[]{:S(2)}) async-start(), calls=%async_computation.10 | async-start | bytes 2359296 | tf_op jit(solution)/shard_map/all_gather | solution.py:95
  8.7 153.4 %all-gather.15.cloned.1.call-start = ((), (), s32[]{:S(2)}) async-start(), calls=%async_computation.8 | async-start | bytes 2359296 | tf_op jit(solution)/shard_map/all_gather | solution.py:97
  9.4 200.5 %all-gather.17.cloned.1.call-start = ((), (), s32[]{:S(2)}) async-start(), calls=%async_computation.9 | async-start | bytes 2621440 | tf_op jit(solution)/shard_map/all_gather | solution.py:132
  165.3 96.2 %all-gather.21.cloned.1.call-start = ((), (), s32[]{:S(2)}) async-start(), calls=%async_computation.11 | async-start | bytes 2359296 | tf_op jit(solution)/shard_map/all_gather | solution.py:98
  165.9 149.0 %all-reduce.11.cloned.1.call-start = ((), (), s32[]{:S(2)}) async-start(), calls=%async_computation.12 | async-start | bytes 4194304 | tf_op jit(solution)/shard_map/psum | solution.py:156
  265.2 177.1 %all-gather.23.cloned.1.call-start = ((), (), s32[]{:S(2)}) async-start(), calls=%async_computation.13 | async-start | bytes 9437184 | tf_op jit(solution)/shard_map/all_gather | solution.py:99
  266.0 301.8 %all-gather.25.cloned.1.call-start = ((), (), s32[]{:S(2)}) async-start(), calls=%async_computation.14 | async-start | bytes 9437184 | tf_op jit(solution)/shard_map/all_gather | solution.py:100
  266.7 426.9 %all-gather.27.cloned.1.call-start = ((), (), s32[]{:S(2)}) async-start(), calls=%async_computation.15 | async-start | bytes 9437184 | tf_op jit(solution)/shard_map/all_gather | solution.py:101
  267.5 502.1 %all-gather.29.cloned.1.call-start = ((), (), s32[]{:S(2)}) async-start(), calls=%async_computation.23 | async-start | bytes 10485760 | tf_op jit(solution)/shard_map/all_gather | solution.py:196
  712.9 300.8 %all-reduce.13.cloned.1.call-start = ((), (), s32[]{:S(2)}) async-start(), calls=%async_computation.24 | async-start | bytes 4194304 | tf_op jit(solution)/shard_map/psum | solution.py:163
  788.0 38.7 %collective-permute-start.1 = (f32[2,256,512]{1,2,0:T(8,128)}, f32[2,256,512]{1,2,0:T(8,128)S(1)}, u32[]{:S(2)}, u32[]{:S(2)}) collective-permute-start(f32[2,256,512]{1,2,0:T(8,128)} %maximum_add_fusion.2), channel_id=1, source_target_pairs={{12,0},{0,4},{4,8},{8,12},{13,1},{1,5},{5,9},{9,13},{14,2},{2,6},{... | collective-permute-start | bytes 3145736 | tf_op jit(solution)/shard_map/while/body/eval_jaxpr/ppermute | solution.py:16
  789.5 37.2 %collective-permute-start = (bf16[2,256,512]{1,2,0:T(8,128)(2,1)S(1)}, bf16[2,256,512]{1,2,0:T(8,128)(2,1)}, u32[]{:S(2)}, u32[]{:S(2)}) collective-permute-start(bf16[2,256,512]{1,2,0:T(8,128)(2,1)S(1)} %copy.94), channel_id=1, source_target_pairs={{12,0},{0,4},{4,8},{8,12},{13,1},{1,5},{5,9},{9,13},{14,2},{2,6},{... | collective-permute-start | bytes 1572872 | tf_op jit(solution)/shard_map/while/body/eval_jaxpr/ppermute | solution.py:16
  833.1 37.8 %collective-permute-start.1 = (f32[2,256,512]{1,2,0:T(8,128)}, f32[2,256,512]{1,2,0:T(8,128)S(1)}, u32[]{:S(2)}, u32[]{:S(2)}) collective-permute-start(f32[2,256,512]{1,2,0:T(8,128)} %maximum_add_fusion.2), channel_id=1, source_target_pairs={{12,0},{0,4},{4,8},{8,12},{13,1},{1,5},{5,9},{9,13},{14,2},{2,6},{... | collective-permute-start | bytes 3145736 | tf_op jit(solution)/shard_map/while/body/eval_jaxpr/ppermute | solution.py:16
  833.1 37.8 %collective-permute-start = (bf16[2,256,512]{1,2,0:T(8,128)(2,1)S(1)}, bf16[2,256,512]{1,2,0:T(8,128)(2,1)}, u32[]{:S(2)}, u32[]{:S(2)}) collective-permute-start(bf16[2,256,512]{1,2,0:T(8,128)(2,1)S(1)} %copy.94), channel_id=1, source_target_pairs={{12,0},{0,4},{4,8},{8,12},{13,1},{1,5},{5,9},{9,13},{14,2},{2,6},{... | collective-permute-start | bytes 1572872 | tf_op jit(solution)/shard_map/while/body/eval_jaxpr/ppermute | solution.py:16
  877.5 36.9 %collective-permute-start.1 = (f32[2,256,512]{1,2,0:T(8,128)}, f32[2,256,512]{1,2,0:T(8,128)S(1)}, u32[]{:S(2)}, u32[]{:S(2)}) collective-permute-start(f32[2,256,512]{1,2,0:T(8,128)} %maximum_add_fusion.2), channel_id=1, source_target_pairs={{12,0},{0,4},{4,8},{8,12},{13,1},{1,5},{5,9},{9,13},{14,2},{2,6},{... | collective-permute-start | bytes 3145736 | tf_op jit(solution)/shard_map/while/body/eval_jaxpr/ppermute | solution.py:16
  877.5 36.9 %collective-permute-start = (bf16[2,256,512]{1,2,0:T(8,128)(2,1)S(1)}, bf16[2,256,512]{1,2,0:T(8,128)(2,1)}, u32[]{:S(2)}, u32[]{:S(2)}) collective-permute-start(bf16[2,256,512]{1,2,0:T(8,128)(2,1)S(1)} %copy.94), channel_id=1, source_target_pairs={{12,0},{0,4},{4,8},{8,12},{13,1},{1,5},{5,9},{9,13},{14,2},{2,6},{... | collective-permute-start | bytes 1572872 | tf_op jit(solution)/shard_map/while/body/eval_jaxpr/ppermute | solution.py:16
  964.7 120.7 %reduce-scatter.14.cloned.1.call-start = ((), (), s32[]{:S(2)}) async-start(), calls=%async_computation.19 | async-start | bytes 2359296 | tf_op jit(solution)/shard_map/reduce_scatter | solution.py:274
  969.3 186.9 %reduce-scatter.8.cloned.1.call-start = ((), (), s32[]{:S(2)}) async-start(), calls=%async_computation.16 | async-start | bytes 2359296 | tf_op jit(solution)/shard_map/reduce_scatter | solution.py:265
  972.7 253.7 %reduce-scatter.10.cloned.1.call-start = ((), (), s32[]{:S(2)}) async-start(), calls=%async_computation.17 | async-start | bytes 2359296 | tf_op jit(solution)/shard_map/reduce_scatter | solution.py:268
  975.2 321.3 %reduce-scatter.12.cloned.1.call-start = ((), (), s32[]{:S(2)}) async-start(), calls=%async_computation.18 | async-start | bytes 2359296 | tf_op jit(solution)/shard_map/reduce_scatter | solution.py:271
  977.5 470.6 %reduce-scatter.16.cloned.1.call-start = ((), (), s32[]{:S(2)}) async-start(), calls=%async_computation.20 | async-start | bytes 9437184 | tf_op jit(solution)/shard_map/reduce_scatter | solution.py:277
  984.4 615.6 %reduce-scatter.18.cloned.1.call-start = ((), (), s32[]{:S(2)}) async-start(), calls=%async_computation.21 | async-start | bytes 9437184 | tf_op jit(solution)/shard_map/reduce_scatter | solution.py:280
  991.3 760.6 %reduce-scatter.20.cloned.1.call-start = ((), (), s32[]{:S(2)}) async-start(), calls=%async_computation.22 | async-start | bytes 9437184 | tf_op jit(solution)/shard_map/reduce_scatter | solution.py:283
  (44 other events, 1265.0 us)
Sparse Core Ops, SparseCore 0:
  10.1 52.0 all-gather.12
  64.3 47.7 all-gather.18
  114.3 47.7 all-gather.14
  165.4 44.4 all-gather.16
  211.7 49.7 all-gather.20
  265.3 49.5 all-reduce.10
  317.3 125.0 all-gather.22
  444.7 123.1 all-gather.24
  570.0 123.5 all-gather.26
  713.0 56.4 all-gather.28
  964.8 48.8 all-reduce.12
  1017.1 68.2 reduce-scatter.13
  1089.5 66.6 reduce-scatter.7
  1159.5 66.7 reduce-scatter.9
  1229.7 66.7 reduce-scatter.11
  1300.0 148.0 reduce-scatter.15
  1452.0 148.0 reduce-scatter.17
  1603.5 148.3 reduce-scatter.19
